TPU v7x, 32 devices: a whole 2x2x4 slice. The times are simulated.
32 devices in a mesh: dev: 32 (over z, y, x, core).
Axes of the slice: x: 2, y: 2, z: 4, core: 2. Of those that a mesh axis runs over, the one named last changes fastest.
Arguments:
- tensor_tiles: bfloat16 [128, 64, 128, 128], P('dev'), may hold values from -196608 to 196608
- tile_coords: int32 [128, 3], P('dev'), may hold values from 0 to 31, as said below
- tile_count: int32 [32], P('dev'), may hold values from 1 to 4, as said below
- owned_i: int32 [32], P('dev'), may hold values from 0 to 31, as said below
- owned_j: int32 [32], P('dev'), may hold values from 0 to 31, as said below
- owned_k: int32 [32], P('dev'), may hold values from 0 to 31, as said below
- factor_a: float32 [32, 64, 512], P('dev'), may hold values from 0 to 7
- factor_b: float32 [32, 128, 512], P('dev'), may hold values from 0 to 7
- factor_c: float32 [32, 128, 512], P('dev'), may hold values from 0 to 7
- dual_a: float32 [32, 64, 512], P('dev'), may hold values from -1.75 to 1.75
- dual_b: float32 [32, 128, 512], P('dev'), may hold values from -1.75 to 1.75
- dual_c: float32 [32, 128, 512], P('dev'), may hold values from -1.75 to 1.75
- penalty: float32 [3], replicated, may hold values from 0.5 to 2
Outputs:
- factor_a_new: float32 [32, 64, 512], P('dev')
- dual_a_new: float32 [32, 64, 512], P('dev')
- factor_b_new: float32 [32, 128, 512], P('dev')
- dual_b_new: float32 [32, 128, 512], P('dev')
- factor_c_new: float32 [32, 128, 512], P('dev')
- dual_c_new: float32 [32, 128, 512], P('dev')
Inputs may be any that keep to these rules, and one draw needn't show every extreme that they name: `owned_i`: each block number appears once. `owned_j`: each block number appears once. `owned_k`: each block number appears once. `tile_coords`: for a live slot on device d, the block named for each mode is owned by a device d + o with o between -2 and 2, counted around the axis; slots may name the same blocks, and their tiles then add; slots that are not live hold arbitrary block numbers. `tile_count`: some device has all 4 slots live.
All inputs are finite; a program needn't handle non-finite values.
Results may differ from a plain program's by a relative error of at most 0.0025.
The roundings to bfloat16 on the way count: a program that leaves them out, or rounds other values in their place, can miss the bound.
Values may be sent and summed in bfloat16 or wider, within the bound.
A program may use at most 128 MiB of HBM per device.

v0:
```python
import jax
import jax.numpy as jnp
from jax import lax
from jax.sharding import PartitionSpec as P

ITERS = 6
REACH = 2


def for_sending(array):
    return jax.tree.map(lambda a: a.astype(jnp.bfloat16) if a.dtype == jnp.float32 else a, array)


def passed_along(block, axis, distance):
    devices = range(lax.axis_size(axis))
    route = [((i - distance) % len(devices), i) for i in devices]
    return lax.ppermute(block, axis, route)


def chol_solve(chol_low, right_side):
    middle = lax.linalg.triangular_solve(chol_low, right_side, left_side=True, lower=True)
    return lax.linalg.triangular_solve(
        chol_low, middle, left_side=True, lower=True, transpose_a=True
    )


def gram_local(factor):
    flat_rows = factor.reshape(-1, factor.shape[-1])
    return lax.dot_general(
        flat_rows,
        flat_rows,
        (((0,), (0,)), ((), ())),
        precision=lax.Precision.HIGHEST,
        preferred_element_type=jnp.float32,
    )


def window_offsets():
    offsets = [0]
    for distance in range(1, REACH + 1):
        offsets.append(distance)
        offsets.append(-distance)
    return offsets


def neighbour(payload, offset):
    return jax.tree.map(
        lambda part, own: part.astype(own.dtype),
        passed_along(for_sending(payload), "dev", -offset),
        payload,
    )


def expand(payload):
    result = [payload]
    for offset in window_offsets()[1:]:
        result.append(neighbour(payload, offset))
    return result


def fold(totals):
    offsets = window_offsets()
    result = totals[0]
    for place_index in range(1, len(offsets)):
        result = result + passed_along(totals[place_index], "dev", offsets[place_index])
    return result


def position(window_ids, block_id):
    return jnp.sum(
        jnp.where(window_ids == block_id, jnp.arange(window_ids.shape[0], dtype=jnp.int32), 0)
    )


def admm_update(mttkrp, factor, dual_var, gram_mat, weight):
    rank_size = gram_mat.shape[0]
    rho_value = weight * jnp.trace(gram_mat) / rank_size
    identity = jnp.eye(rank_size, dtype=jnp.float32)
    chol_low = jnp.linalg.cholesky(gram_mat + rho_value * identity)
    inverse = chol_solve(chol_low, identity)
    for sweep_index in range(ITERS):
        auxiliary = jnp.dot(
            mttkrp + rho_value * (factor + dual_var),
            inverse,
            precision=lax.Precision.HIGHEST,
            preferred_element_type=jnp.float32,
        )
        factor = jnp.maximum(auxiliary - dual_var, 0.0)
        dual_var = dual_var + factor - auxiliary
    return (factor, dual_var)


def per_device(
    tensor_tiles,
    tile_coords,
    tile_count,
    owned_i,
    owned_j,
    owned_k,
    factor_a,
    factor_b,
    factor_c,
    dual_a,
    dual_b,
    dual_c,
    penalty,
):
    slot_count, rows_first, rows_second, rows_third = tensor_tiles.shape
    rank_size = factor_a.shape[2]
    count_live = tile_count[0]
    win_count = len(window_offsets())
    gram_b, gram_c = lax.psum((gram_local(factor_b), gram_local(factor_c)), "dev")
    own_ids = jnp.concatenate([owned_i, owned_j, owned_k])
    first_window = expand(
        (factor_b[0].astype(jnp.bfloat16), factor_c[0].astype(jnp.bfloat16), own_ids)
    )
    win_b = jnp.stack([member[0] for member in first_window])
    win_c = jnp.stack([member[1] for member in first_window])
    ids_window = jnp.stack([member[2] for member in first_window])

    def slice_tile(slot_index):
        return lax.dynamic_index_in_dim(tensor_tiles, slot_index, 0, keepdims=False)

    def first_part(tile_now, coord_row):
        third_rows = win_c[position(ids_window[:, 2], coord_row[2])]
        flat_tile = tile_now.reshape(rows_first * rows_second, rows_third)
        partial_value = jnp.dot(flat_tile, third_rows, preferred_element_type=jnp.float32)
        return partial_value.reshape(rows_first, rows_second, rank_size)

    def mode_first(slot_index, loop_carry):
        totals = loop_carry[0]
        coord_row = tile_coords[slot_index]
        partial_value = first_part(slice_tile(slot_index), coord_row)
        second_rows = win_b[position(ids_window[:, 1], coord_row[1])]
        contrib = jnp.sum(partial_value * second_rows[None, :, :], axis=1)
        totals = totals.at[position(ids_window[:, 0], coord_row[0])].add(contrib)
        return (totals,)

    start_first = jnp.zeros((win_count, rows_first, rank_size), jnp.float32)
    first_carry = (start_first,)
    first_result = lax.fori_loop(0, count_live, mode_first, first_carry)
    mttkrp_a = fold(first_result[0])
    factor_a_new, dual_a_new = admm_update(
        mttkrp_a, factor_a[0], dual_a[0], gram_b * gram_c, penalty[0]
    )
    gram_a = lax.psum(gram_local(factor_a_new), "dev")
    second_window = expand((factor_a_new.astype(jnp.bfloat16),))
    win_a = jnp.stack([member[0] for member in second_window])

    def mode_second(slot_index, loop_carry):
        totals = loop_carry[0]
        coord_row = tile_coords[slot_index]
        partial_value = first_part(slice_tile(slot_index), coord_row)
        first_rows = win_a[position(ids_window[:, 0], coord_row[0])]
        contrib = jnp.sum(partial_value * first_rows[:, None, :], axis=0)
        totals = totals.at[position(ids_window[:, 1], coord_row[1])].add(contrib)
        return (totals,) + tuple(loop_carry[1:])

    second_carry = (jnp.zeros((win_count, rows_second, rank_size), jnp.float32),) + tuple(
        first_result[1:]
    )
    second_result = lax.fori_loop(0, count_live, mode_second, second_carry)
    mttkrp_b = fold(second_result[0])
    factor_b_new, dual_b_new = admm_update(
        mttkrp_b, factor_b[0], dual_b[0], gram_a * gram_c, penalty[1]
    )
    gram_bn = lax.psum(gram_local(factor_b_new), "dev")
    third_window = expand((factor_b_new.astype(jnp.bfloat16),))
    win_bn = jnp.stack([member[0] for member in third_window])

    def mode_third(slot_index, loop_carry):
        totals = loop_carry[0]
        coord_row = tile_coords[slot_index]
        tile_now = slice_tile(slot_index)
        first_rows = win_a[position(ids_window[:, 0], coord_row[0])]
        flat_tile = tile_now.reshape(rows_first, rows_second * rows_third)
        crossed = lax.dot_general(
            flat_tile, first_rows, (((0,), (0,)), ((), ())), preferred_element_type=jnp.float32
        )
        crossed = crossed.reshape(rows_second, rows_third, rank_size)
        second_rows = win_bn[position(ids_window[:, 1], coord_row[1])]
        contrib = jnp.sum(crossed * second_rows[:, None, :], axis=0)
        totals = totals.at[position(ids_window[:, 2], coord_row[2])].add(contrib)
        return (totals,)

    third_result = lax.fori_loop(
        0, count_live, mode_third, (jnp.zeros((win_count, rows_third, rank_size), jnp.float32),)
    )
    mttkrp_c = fold(third_result[0])
    factor_c_new, dual_c_new = admm_update(
        mttkrp_c, factor_c[0], dual_c[0], gram_a * gram_bn, penalty[2]
    )
    return (
        factor_a_new[None],
        dual_a_new[None],
        factor_b_new[None],
        dual_b_new[None],
        factor_c_new[None],
        dual_c_new[None],
    )


def solution(mesh):
    return jax.shard_map(
        per_device,
        mesh=mesh,
        in_specs=(
            P("dev", None, None, None),
            P("dev", None),
            P("dev"),
            P("dev"),
            P("dev"),
            P("dev"),
            P("dev", None, None),
            P("dev", None, None),
            P("dev", None, None),
            P("dev", None, None),
            P("dev", None, None),
            P("dev", None, None),
            P(),
        ),
        out_specs=(
            P("dev", None, None),
            P("dev", None, None),
            P("dev", None, None),
            P("dev", None, None),
            P("dev", None, None),
            P("dev", None, None),
        ),
        check_vma=False,
    )
```

profile of v0, /device:TPU:0, one launch (start us, length us, event | category | flops | bytes accessed | tf_op | source)
XLA Modules:
  0.0 1005.6 jit_solution(10114383606782808656)
XLA Ops:
  18.6 8.4 collective-permute-start.4
  56.0 61.0 %while.45 = (s32[]{:T(128)}, f32[5,64,512]{2,1,0:T(8,128)S(1)}, s32[]{:T(128)}, s32[5,3]{0,1:T(4,128)S(1)}, s32[4,3]{1,0:T(4,128)S(1)}, /*index=5*/bf16[4,64,128...) while((s32[]{:T(128)}, f32[5,64,512]{2,1,0:T(8,128)S(1)}, ...), condition=%wide.region_6.7_spmd, body=%wide.region_0.6_spmd.sunk | while | flops 1082228736 | bytes 3408315 | solution.py:141
  132.5 36.2 %all-reduce.10.cloned.1.call-done = (f32[512,512]{0,1:T(8,128)}, f32[512,512]{0,1:T(8,128)}) async-done(((f32[512,512]{0,1:T(8,128)}, f32[512,512]{0,1:T(8,128)}), (f32[512,512]{0,1:T(8,128)}, f32[512,512]{0,1:T(8,128)})) %all-reduce.10.cloned.1.call-update) | async-done | bytes 2097168 | tf_op jit(solution)/shard_map/psum | solution.py:112
  176.3 11.7 %cholesky.374 = f32[128,128]{1,0:T(8,128)S(1)} custom-call(f32[128,128]{1,0:T(8,128)S(1)} %cholesky.586), custom_call_target="Cholesky" | custom-call | tf_op jit(solution)/shard_map/jit(cholesky)/cholesky | solution.py:79
  188.0 9.8 custom-call.36
  200.5 11.7 %cholesky.393 = f32[128,128]{1,0:T(8,128)S(1)} custom-call(f32[128,128]{1,0:T(8,128)S(1)} %cholesky.590), custom_call_target="Cholesky" | custom-call | tf_op jit(solution)/shard_map/jit(cholesky)/cholesky | solution.py:79
  212.2 10.2 %custom-call.37 = f32[1,128,128]{1,2,0:T(8,128)S(1)} custom-call(f32[1,128,128]{2,1,0:T(8,128)S(1)} %get-tuple-element.423), custom_call_target="InvertDiagBlocksLowerTriangular" | custom-call | tf_op jit(solution)/shard_map/jit(cholesky)/cholesky | solution.py:79
  224.0 11.7 %cholesky.414 = f32[128,128]{1,0:T(8,128)S(1)} custom-call(f32[128,128]{1,0:T(8,128)S(1)} %cholesky.595), custom_call_target="Cholesky" | custom-call | tf_op jit(solution)/shard_map/jit(cholesky)/cholesky | solution.py:79
  236.4 9.8 custom-call.38
  247.7 11.7 %cholesky.431 = f32[128,128]{1,0:T(8,128)S(1)} custom-call(f32[128,128]{1,0:T(8,128)S(1)} %convolution_subtract_fusion.26), custom_call_target="Cholesky" | custom-call | tf_op jit(solution)/shard_map/jit(cholesky)/cholesky | solution.py:79
  271.5 39.5 %custom-call.40 = f32[4,128,128]{1,2,0:T(8,128)S(1)} custom-call(f32[4,128,128]{2,1,0:T(8,128)S(1)} %get-tuple-element.218), custom_call_target="InvertDiagBlocksLowerTriangular" | custom-call | tf_op jit(solution)/shard_map/triangular_solve/custom-call.8 | solution.py:22
  336.9 60.9 %while.46 = (s32[]{:T(128)}, f32[5,128,512]{2,1,0:T(8,128)S(1)}, s32[]{:T(128)}, s32[5,3]{0,1:T(4,128)S(1)}, s32[4,3]{1,0:T(4,128)S(1)}, /*index=5*/bf16[4,64,12...) while((s32[]{:T(128)}, f32[5,128,512]{2,1,0:T(8,128)S(1)}, ...), condition=%wide.region_24.28_spmd, body=%wide.region_18.27_spmd.sunk | while | flops 1082228736 | bytes 3604923 | solution.py:162
  419.1 120.2 %all-reduce.6.cloned.1.call-done = f32[512,512]{0,1:T(8,128)} async-done(((f32[512,512]{0,1:T(8,128)}), f32[512,512]{0,1:T(8,128)}) %all-reduce.6.cloned.1.call-update) | async-done | bytes 1048592 | tf_op jit(solution)/shard_map/psum | solution.py:146
  546.5 11.7 %cholesky.446 = f32[128,128]{1,0:T(8,128)S(1)} custom-call(f32[128,128]{1,0:T(8,128)S(1)} %cholesky.599), custom_call_target="Cholesky" | custom-call | tf_op jit(solution)/shard_map/jit(cholesky)/cholesky | solution.py:79
  558.3 9.8 custom-call.41
  570.7 11.7 %cholesky.465 = f32[128,128]{1,0:T(8,128)S(1)} custom-call(f32[128,128]{1,0:T(8,128)S(1)} %cholesky.603), custom_call_target="Cholesky" | custom-call | tf_op jit(solution)/shard_map/jit(cholesky)/cholesky | solution.py:79
  583.7 10.0 custom-call.42
  595.2 11.7 %cholesky.486 = f32[128,128]{1,0:T(8,128)S(1)} custom-call(f32[128,128]{1,0:T(8,128)S(1)} %cholesky.608), custom_call_target="Cholesky" | custom-call | tf_op jit(solution)/shard_map/jit(cholesky)/cholesky | solution.py:79
  607.6 9.8 custom-call.43
  618.9 12.1 %cholesky.503 = f32[128,128]{1,0:T(8,128)S(1)} custom-call(f32[128,128]{1,0:T(8,128)S(1)} %convolution_subtract_fusion.25), custom_call_target="Cholesky" | custom-call | tf_op jit(solution)/shard_map/jit(cholesky)/cholesky | solution.py:79
  642.5 39.3 %custom-call.45 = f32[4,128,128]{1,2,0:T(8,128)S(1)} custom-call(f32[4,128,128]{2,1,0:T(8,128)S(1)} %get-tuple-element.220), custom_call_target="InvertDiagBlocksLowerTriangular" | custom-call | tf_op jit(solution)/shard_map/triangular_solve/custom-call.8 | solution.py:22
  707.1 80.1 %while.47 = (s32[]{:T(128)}, f32[5,128,512]{2,1,0:T(8,128)S(1)}, s32[]{:T(128)}, s32[5,3]{0,1:T(4,128)S(1)}, s32[4,3]{1,0:T(4,128)S(1)}, /*index=5*/bf16[4,64,12...) while((s32[]{:T(128)}, f32[5,128,512]{2,1,0:T(8,128)S(1)}, ...), condition=%wide.region_33.37_spmd, body=%wide.region_27.36_spmd.sunk | while | flops 1090650112 | bytes 8061371 | solution.py:186
  807.1 35.2 %all-reduce.8.cloned.1.call-done = f32[512,512]{0,1:T(8,128)} async-done(((f32[512,512]{0,1:T(8,128)}), f32[512,512]{0,1:T(8,128)}) %all-reduce.8.cloned.1.call-update) | async-done | bytes 1048592 | tf_op jit(solution)/shard_map/psum | solution.py:167
  849.6 11.7 %cholesky.518 = f32[128,128]{1,0:T(8,128)S(1)} custom-call(f32[128,128]{1,0:T(8,128)S(1)} %cholesky.612), custom_call_target="Cholesky" | custom-call | tf_op jit(solution)/shard_map/jit(cholesky)/cholesky | solution.py:79
  861.4 9.8 custom-call.46
  873.8 11.7 %cholesky.537 = f32[128,128]{1,0:T(8,128)S(1)} custom-call(f32[128,128]{1,0:T(8,128)S(1)} %cholesky.616), custom_call_target="Cholesky" | custom-call | tf_op jit(solution)/shard_map/jit(cholesky)/cholesky | solution.py:79
  886.9 10.2 %custom-call.47 = f32[1,128,128]{1,2,0:T(8,128)S(1)} custom-call(f32[1,128,128]{2,1,0:T(8,128)S(1)} %get-tuple-element.403), custom_call_target="InvertDiagBlocksLowerTriangular" | custom-call | tf_op jit(solution)/shard_map/jit(cholesky)/cholesky | solution.py:79
  898.7 11.7 %cholesky.558 = f32[128,128]{1,0:T(8,128)S(1)} custom-call(f32[128,128]{1,0:T(8,128)S(1)} %cholesky.621), custom_call_target="Cholesky" | custom-call | tf_op jit(solution)/shard_map/jit(cholesky)/cholesky | solution.py:79
  911.0 9.8 custom-call.48
  922.3 11.8 %cholesky.575 = f32[128,128]{1,0:T(8,128)S(1)} custom-call(f32[128,128]{1,0:T(8,128)S(1)} %convolution_subtract_fusion.24), custom_call_target="Cholesky" | custom-call | tf_op jit(solution)/shard_map/jit(cholesky)/cholesky | solution.py:79
  937.7 8.5 while.50
  946.1 39.3 %custom-call.50 = f32[4,128,128]{1,2,0:T(8,128)S(1)} custom-call(f32[4,128,128]{2,1,0:T(8,128)S(1)} %get-tuple-element.222), custom_call_target="InvertDiagBlocksLowerTriangular" | custom-call | tf_op jit(solution)/shard_map/triangular_solve/custom-call.8 | solution.py:22
  (429 shorter events, 364.4 us)
Async XLA Ops:
  7.2 161.5 %all-reduce.10.cloned.1.call-start = ((), (), s32[]{:S(2)}) async-start(), calls=%async_computation.2 | async-start | bytes 4194304 | tf_op jit(solution)/shard_map/psum | solution.py:112
  9.2 25.0 %collective-permute-start = (s32[3]{0:T(128)S(1)}, s32[3]{0:T(128)S(1)}, u32[]{:S(2)}, u32[]{:S(2)}) collective-permute-start(s32[3]{0:T(128)S(1)} %pad_add_fusion), channel_id=1, source_target_pairs={{1,0},{2,1},{3,2},{4,3},{5,4},{6,5},{7,6},{8,7},{9,8},{10,9},{11,1... | collective-permute-start | bytes 44 | tf_op jit(solution)/shard_map/ppermute | solution.py:17
  15.6 18.6 %collective-permute-start.1 = (s32[3]{0:T(128)S(1)}, s32[3]{0:T(128)S(1)}, u32[]{:S(2)}, u32[]{:S(2)}) collective-permute-start(s32[3]{0:T(128)S(1)} %pad_add_fusion), channel_id=1, source_target_pairs={{31,0},{0,1},{1,2},{2,3},{3,4},{4,5},{5,6},{6,7},{7,8},{8,9},{9,10... | collective-permute-start | bytes 44 | tf_op jit(solution)/shard_map/ppermute | solution.py:17
  15.6 19.0 %collective-permute-start.2 = (s32[3]{0:T(128)S(1)}, s32[3]{0:T(128)S(1)}, u32[]{:S(2)}, u32[]{:S(2)}) collective-permute-start(s32[3]{0:T(128)S(1)} %pad_add_fusion), channel_id=1, source_target_pairs={{2,0},{3,1},{4,2},{5,3},{6,4},{7,5},{8,6},{9,7},{10,8},{11,9},{12,... | collective-permute-start | bytes 44 | tf_op jit(solution)/shard_map/ppermute | solution.py:17
  16.7 19.6 %collective-permute-start.3 = (s32[3]{0:T(128)S(1)}, s32[3]{0:T(128)S(1)}, u32[]{:S(2)}, u32[]{:S(2)}) collective-permute-start(s32[3]{0:T(128)S(1)} %pad_add_fusion), channel_id=1, source_target_pairs={{30,0},{31,1},{0,2},{1,3},{2,4},{3,5},{4,6},{5,7},{6,8},{7,9},{8,1... | collective-permute-start | bytes 44 | tf_op jit(solution)/shard_map/ppermute | solution.py:17
  18.6 26.1 %collective-permute-start.4 = (bf16[128,512]{1,0:T(8,128)(2,1)S(1)}, bf16[128,512]{1,0:T(8,128)(2,1)S(1)}, u32[]{:S(2)}, u32[]{:S(2)}) collective-permute-start(bf16[128,512]{1,0:T(8,128)(2,1)S(1)} %bitcast_convert_fusion.4), channel_id=1, source_target_pairs={{1,0},{2,1},{3,2},{4,3},{5,4},{6,5},{7,6},{8,7},{9,8},{10,9},{11,1... | collective-permute-start | bytes 393224 | tf_op jit(solution)/shard_map/ppermute | solution.py:17
  33.3 506.0 %all-reduce.6.cloned.1.call-start = ((), (), s32[]{:S(2)}) async-start(), calls=%async_computation | async-start | bytes 2097152 | tf_op jit(solution)/shard_map/psum | solution.py:146
  34.2 11.1 %collective-permute-start.5 = (bf16[128,512]{1,0:T(8,128)(2,1)S(1)}, bf16[128,512]{1,0:T(8,128)(2,1)S(1)}, u32[]{:S(2)}, u32[]{:S(2)}) collective-permute-start(bf16[128,512]{1,0:T(8,128)(2,1)S(1)} %bitcast_convert_fusion.4), channel_id=1, source_target_pairs={{31,0},{0,1},{1,2},{2,3},{3,4},{4,5},{5,6},{6,7},{7,8},{8,9},{9,10... | collective-permute-start | bytes 393224 | tf_op jit(solution)/shard_map/ppermute | solution.py:17
  34.2 11.1 %collective-permute-start.6 = (bf16[128,512]{1,0:T(8,128)(2,1)S(1)}, bf16[128,512]{1,0:T(8,128)(2,1)S(1)}, u32[]{:S(2)}, u32[]{:S(2)}) collective-permute-start(bf16[128,512]{1,0:T(8,128)(2,1)S(1)} %bitcast_convert_fusion.4), channel_id=1, source_target_pairs={{2,0},{3,1},{4,2},{5,3},{6,4},{7,5},{8,6},{9,7},{10,8},{11,9},{12,... | collective-permute-start | bytes 393224 | tf_op jit(solution)/shard_map/ppermute | solution.py:17
  34.6 12.8 %collective-permute-start.7 = (bf16[128,512]{1,0:T(8,128)(2,1)S(1)}, bf16[128,512]{1,0:T(8,128)(2,1)S(1)}, u32[]{:S(2)}, u32[]{:S(2)}) collective-permute-start(bf16[128,512]{1,0:T(8,128)(2,1)S(1)} %bitcast_convert_fusion.4), channel_id=1, source_target_pairs={{30,0},{31,1},{0,2},{1,3},{2,4},{3,5},{4,6},{5,7},{6,8},{7,9},{8,1... | collective-permute-start | bytes 393224 | tf_op jit(solution)/shard_map/ppermute | solution.py:17
  36.3 11.4 %collective-permute-start.8 = (bf16[128,512]{1,0:T(8,128)(2,1)S(1)}, bf16[128,512]{1,0:T(8,128)(2,1)S(1)}, u32[]{:S(2)}, u32[]{:S(2)}) collective-permute-start(bf16[128,512]{1,0:T(8,128)(2,1)S(1)} %bitcast_convert_fusion.3), channel_id=1, source_target_pairs={{1,0},{2,1},{3,2},{4,3},{5,4},{6,5},{7,6},{8,7},{9,8},{10,9},{11,1... | collective-permute-start | bytes 393224 | tf_op jit(solution)/shard_map/ppermute | solution.py:17
  44.7 10.2 %collective-permute-start.9 = (bf16[128,512]{1,0:T(8,128)(2,1)S(1)}, bf16[128,512]{1,0:T(8,128)(2,1)S(1)}, u32[]{:S(2)}, u32[]{:S(2)}) collective-permute-start(bf16[128,512]{1,0:T(8,128)(2,1)S(1)} %bitcast_convert_fusion.3), channel_id=1, source_target_pairs={{31,0},{0,1},{1,2},{2,3},{3,4},{4,5},{5,6},{6,7},{7,8},{8,9},{9,10... | collective-permute-start | bytes 393224 | tf_op jit(solution)/shard_map/ppermute | solution.py:17
  45.3 9.6 collective-permute-start.10
  45.3 10.5 %collective-permute-start.11 = (bf16[128,512]{1,0:T(8,128)(2,1)S(1)}, bf16[128,512]{1,0:T(8,128)(2,1)S(1)}, u32[]{:S(2)}, u32[]{:S(2)}) collective-permute-start(bf16[128,512]{1,0:T(8,128)(2,1)S(1)} %bitcast_convert_fusion.3), channel_id=1, source_target_pairs={{30,0},{31,1},{0,2},{1,3},{2,4},{3,5},{4,6},{5,7},{6,8},{7,9},{8,1... | collective-permute-start | bytes 393224 | tf_op jit(solution)/shard_map/ppermute | solution.py:17
  117.9 11.3 %collective-permute-start.12 = (f32[64,512]{1,0:T(8,128)S(1)}, f32[64,512]{1,0:T(8,128)S(1)}, u32[]{:S(2)}, u32[]{:S(2)}) collective-permute-start(f32[64,512]{1,0:T(8,128)S(1)} %get-tuple-element.389), channel_id=1, source_target_pairs={{31,0},{0,1},{1,2},{2,3},{3,4},{4,5},{5,6},{6,7},{7,8},{8,9},{9,10... | collective-permute-start | bytes 393224 | tf_op jit(solution)/shard_map/ppermute | solution.py:17
  118.0 11.2 %collective-permute-start.13 = (f32[64,512]{1,0:T(8,128)S(1)}, f32[64,512]{1,0:T(8,128)S(1)}, u32[]{:S(2)}, u32[]{:S(2)}) collective-permute-start(f32[64,512]{1,0:T(8,128)S(1)} %get-tuple-element.392), channel_id=1, source_target_pairs={{1,0},{2,1},{3,2},{4,3},{5,4},{6,5},{7,6},{8,7},{9,8},{10,9},{11,1... | collective-permute-start | bytes 393224 | tf_op jit(solution)/shard_map/ppermute | solution.py:17
  123.3 9.1 collective-permute-start.14
  123.3 9.1 collective-permute-start.15
  326.8 7.3 collective-permute-start.18
  328.8 7.9 collective-permute-start.19
  399.5 13.1 %collective-permute-start.20 = (f32[128,512]{1,0:T(8,128)}, f32[128,512]{1,0:T(8,128)}, u32[]{:S(2)}, u32[]{:S(2)}) collective-permute-start(f32[128,512]{1,0:T(8,128)} %get-tuple-element.383), channel_id=1, source_target_pairs={{31,0},{0,1},{1,2},{2,3},{3,4},{4,5},{5,6},{6,7},{7,8},{8,9},{9,10... | collective-permute-start | bytes 786440 | tf_op jit(solution)/shard_map/ppermute | solution.py:17
  399.5 13.1 %collective-permute-start.21 = (f32[128,512]{1,0:T(8,128)}, f32[128,512]{1,0:T(8,128)}, u32[]{:S(2)}, u32[]{:S(2)}) collective-permute-start(f32[128,512]{1,0:T(8,128)} %get-tuple-element.386), channel_id=1, source_target_pairs={{1,0},{2,1},{3,2},{4,3},{5,4},{6,5},{7,6},{8,7},{9,8},{10,9},{11,1... | collective-permute-start | bytes 786440 | tf_op jit(solution)/shard_map/ppermute | solution.py:17
  404.9 10.3 %collective-permute-start.22 = (f32[128,512]{1,0:T(8,128)}, f32[128,512]{1,0:T(8,128)}, u32[]{:S(2)}, u32[]{:S(2)}) collective-permute-start(f32[128,512]{1,0:T(8,128)} %get-tuple-element.385), channel_id=1, source_target_pairs={{30,0},{31,1},{0,2},{1,3},{2,4},{3,5},{4,6},{5,7},{6,8},{7,9},{8,1... | collective-permute-start | bytes 786440 | tf_op jit(solution)/shard_map/ppermute | solution.py:17
  404.9 12.2 %collective-permute-start.23 = (f32[128,512]{1,0:T(8,128)}, f32[128,512]{1,0:T(8,128)}, u32[]{:S(2)}, u32[]{:S(2)}) collective-permute-start(f32[128,512]{1,0:T(8,128)} %get-tuple-element.384), channel_id=1, source_target_pairs={{2,0},{3,1},{4,2},{5,3},{6,4},{7,5},{8,6},{9,7},{10,8},{11,9},{12,... | collective-permute-start | bytes 786440 | tf_op jit(solution)/shard_map/ppermute | solution.py:17
  412.5 429.8 %all-reduce.8.cloned.1.call-start = ((), (), s32[]{:S(2)}) async-start(), calls=%async_computation.1 | async-start | bytes 2097152 | tf_op jit(solution)/shard_map/psum | solution.py:167
  696.3 8.0 collective-permute-start.25
  696.3 8.0 collective-permute-start.26
  698.3 8.7 collective-permute-start.27
  787.4 12.6 %collective-permute-start.28 = (f32[128,512]{1,0:T(8,128)S(1)}, f32[128,512]{1,0:T(8,128)S(1)}, u32[]{:S(2)}, u32[]{:S(2)}) collective-permute-start(f32[128,512]{1,0:T(8,128)S(1)} %get-tuple-element.379), channel_id=1, source_target_pairs={{31,0},{0,1},{1,2},{2,3},{3,4},{4,5},{5,6},{6,7},{7,8},{8,9},{9,10... | collective-permute-start | bytes 786440 | tf_op jit(solution)/shard_map/ppermute | solution.py:17
  787.4 12.6 %collective-permute-start.29 = (f32[128,512]{1,0:T(8,128)S(1)}, f32[128,512]{1,0:T(8,128)S(1)}, u32[]{:S(2)}, u32[]{:S(2)}) collective-permute-start(f32[128,512]{1,0:T(8,128)S(1)} %get-tuple-element.382), channel_id=1, source_target_pairs={{1,0},{2,1},{3,2},{4,3},{5,4},{6,5},{7,6},{8,7},{9,8},{10,9},{11,1... | collective-permute-start | bytes 786440 | tf_op jit(solution)/shard_map/ppermute | solution.py:17
  792.8 10.3 %collective-permute-start.30 = (f32[128,512]{1,0:T(8,128)S(1)}, f32[128,512]{1,0:T(8,128)S(1)}, u32[]{:S(2)}, u32[]{:S(2)}) collective-permute-start(f32[128,512]{1,0:T(8,128)S(1)} %get-tuple-element.381), channel_id=1, source_target_pairs={{30,0},{31,1},{0,2},{1,3},{2,4},{3,5},{4,6},{5,7},{6,8},{7,9},{8,1... | collective-permute-start | bytes 786440 | tf_op jit(solution)/shard_map/ppermute | solution.py:17
  792.8 13.5 %collective-permute-start.31 = (f32[128,512]{1,0:T(8,128)S(1)}, f32[128,512]{1,0:T(8,128)S(1)}, u32[]{:S(2)}, u32[]{:S(2)}) collective-permute-start(f32[128,512]{1,0:T(8,128)S(1)} %get-tuple-element.380), channel_id=1, source_target_pairs={{2,0},{3,1},{4,2},{5,3},{6,4},{7,5},{8,6},{9,7},{10,8},{11,9},{12,... | collective-permute-start | bytes 786440 | tf_op jit(solution)/shard_map/ppermute | solution.py:17
  (33 other events, 646.0 us)
Sparse Core Ops, SparseCore 0:
  33.4 135.2 all-reduce.9
  412.6 126.6 all-reduce.5
  700.6 141.6 all-reduce.7
where the time goes:
time: 1010 us
  other arithmetic  422 us (42%)
  waiting for transfers between devices  229 us (23%)
  matrix products  125 us (12%)
  loops' own time  79.9 us (8%)
  starting transfers between devices  70.1 us (7%)
  local copies, waits for them, and re-layouts  50.6 us (5%)
  between operations  29 us (3%)
    another operation x44, other arithmetic, admm_update(): chol_low = jnp.linalg.cholesky(gram_mat + rho_value * identity)  238 us
    psum x1, waiting for transfers between devices, per_device(): gram_a = lax.psum(gram_local(factor_a_new), 'dev')  120 us
    another operation x7, other arithmetic, chol_solve(): lax.linalg.triangular_solve(chol_low, middle, left_side=True, lower=True,...  119 us
    ppermute x32, starting transfers between devices, passed_along(): return lax.ppermute(block, axis, route)  70 us
    ppermute x32, waiting for transfers between devices, passed_along(): return lax.ppermute(block, axis, route)  37.2 us
    psum x1, waiting for transfers between devices, per_device(): lax.psum((gram_local(factor_b), gram_local(factor_c)), 'dev')  36.2 us
    psum x1, waiting for transfers between devices, per_device(): gram_bn = lax.psum(gram_local(factor_b_new), 'dev')  35.2 us
    reduce_sum x12, other arithmetic, position(): jnp.sum(jnp.where(window_ids == block_id, jnp.arange(window_ids.shape[0],...  31.9 us
  transfers between devices with their start and end apart: 35, of which 16 were waited for; matrix products, arithmetic and copies ran while one was open for 10% of the time, Pallas kernels for 0%

commit v1 on v0

v1 whole, which is shorter than its diff:
```python
import functools

import jax
import jax.numpy as jnp
from jax import lax
from jax.experimental import pallas as pl
from jax.experimental.pallas import tpu as pltpu
from jax.sharding import PartitionSpec as P

ITERS = 6
REACH = 2
LANES = 128
MESH_ID = pl.DeviceIdType.MESH
HIGHEST = lax.Precision.HIGHEST
VMEM_SPEC = pl.BlockSpec(memory_space=pltpu.VMEM)
SMEM_SPEC = pl.BlockSpec(memory_space=pltpu.SMEM)
VMEM_BYTES = 56 * 1024 * 1024


def window_offsets():
    offsets = [0]
    for distance in range(1, REACH + 1):
        offsets.append(distance)
        offsets.append(-distance)
    return offsets


OFFSETS = window_offsets()


def block_pairs(rank):
    count = rank // LANES
    return [(i, j) for i in range(count) for j in range(i, count)]


def packed_rows(rank, matrices, devices):
    unit = 8 * devices
    return -(-matrices * len(block_pairs(rank)) * LANES // unit) * unit


def f32_dot(left, right):
    return jnp.dot(left, right, precision=HIGHEST, preferred_element_type=jnp.float32)


def bf_dot(left, right):
    return jnp.dot(left, right, preferred_element_type=jnp.float32)


def write_gram(out_ref, start, factor):
    rank = factor.shape[1]
    turned = factor.T
    place = start
    for i in range(rank // LANES):
        band = f32_dot(turned[i * LANES : (i + 1) * LANES, :], factor[:, i * LANES :])
        for j in range(i, rank // LANES):
            out_ref[place : place + LANES, :] = band[:, (j - i) * LANES : (j - i + 1) * LANES]
            place += LANES
    return place


def gram_pair_kernel(b_ref, c_ref, gram_ref, low_b_ref, low_c_ref):
    place = write_gram(gram_ref, 0, b_ref[0])
    place = write_gram(gram_ref, place, c_ref[0])
    if place < gram_ref.shape[0]:
        gram_ref[place:, :] = jnp.zeros((gram_ref.shape[0] - place, LANES), jnp.float32)
    low_b_ref[...] = b_ref[0].astype(jnp.bfloat16)
    low_c_ref[...] = c_ref[0].astype(jnp.bfloat16)


def greet(devices, me, with_cube):
    others = []
    if with_cube:
        for t in range(devices.bit_length() - 1):
            bit = (me // (1 << t)) % 2
            others.append(me + (1 - 2 * bit) * (1 << t))
    for offset in OFFSETS[1:]:
        others.append((me + offset + devices) % devices)
    barrier = pltpu.get_barrier_semaphore()
    for other in others:
        pl.semaphore_signal(barrier, inc=1, device_id=(other,), device_id_type=MESH_ID)
    pl.semaphore_wait(barrier, len(others))


def share_kernel(devices, payloads, *refs):
    gram_ref = refs[0]
    own_refs = refs[1 : 1 + payloads]
    sum_ref = refs[1 + payloads]
    win_refs = refs[2 + payloads : 2 + 2 * payloads]
    box_ref, part_ref, win_send, win_recv, local_sem, cube_send, cube_recv = refs[2 + 2 * payloads :]
    me = lax.axis_index("dev")
    greet(devices, me, True)
    window_copies = []
    for place in range(1, len(OFFSETS)):
        target = (me - OFFSETS[place] + devices) % devices
        for q in range(payloads):
            copy = pltpu.make_async_remote_copy(
                src_ref=own_refs[q],
                dst_ref=win_refs[q].at[place],
                send_sem=win_send.at[q, place],
                recv_sem=win_recv.at[q, place],
                device_id=(target,),
                device_id_type=MESH_ID,
            )
            copy.start()
            window_copies.append(copy)
    for q in range(payloads):
        own = pltpu.make_async_copy(own_refs[q], win_refs[q].at[0], local_sem.at[q])
        own.start()
        window_copies.append(own)

    steps = devices.bit_length() - 1
    length = gram_ref.shape[0]
    start = 0
    box = 0
    for t in range(steps):
        half = length // 2
        bit = (me // (1 << t)) % 2
        partner = me + (1 - 2 * bit) * (1 << t)
        keep = pl.multiple_of(start + bit * half, 8)
        give = pl.multiple_of(start + (1 - bit) * half, 8)
        source = gram_ref if t == 0 else part_ref
        target = sum_ref if t == steps - 1 else part_ref
        copy = pltpu.make_async_remote_copy(
            src_ref=source.at[pl.ds(give, half)],
            dst_ref=box_ref.at[pl.ds(box, half)],
            send_sem=cube_send.at[t],
            recv_sem=cube_recv.at[t],
            device_id=(partner,),
            device_id_type=MESH_ID,
        )
        copy.start()
        copy.wait()
        target[pl.ds(keep, half), :] = source[pl.ds(keep, half), :] + box_ref[pl.ds(box, half), :]
        box += half
        start = keep
        length = half
    for t in reversed(range(steps)):
        bit = (me // (1 << t)) % 2
        partner = me + (1 - 2 * bit) * (1 << t)
        piece = pl.ds(pl.multiple_of(start, 8), length)
        copy = pltpu.make_async_remote_copy(
            src_ref=sum_ref.at[piece],
            dst_ref=sum_ref.at[piece],
            send_sem=cube_send.at[steps + t],
            recv_sem=cube_recv.at[steps + t],
            device_id=(partner,),
            device_id_type=MESH_ID,
        )
        copy.start()
        copy.wait()
        start = start - bit * length
        length = 2 * length
    for copy in window_copies:
        copy.wait()


def share(devices, call_id, gram, payload):
    steps = devices.bit_length() - 1
    win = len(OFFSETS)
    count = len(payload)
    result = pl.pallas_call(
        functools.partial(share_kernel, devices, count),
        out_shape=[jax.ShapeDtypeStruct(gram.shape, jnp.float32)]
        + [jax.ShapeDtypeStruct((win,) + p.shape, p.dtype) for p in payload],
        in_specs=[VMEM_SPEC] * (1 + count),
        out_specs=[VMEM_SPEC] * (1 + count),
        scratch_shapes=[
            pltpu.VMEM(gram.shape, jnp.float32),
            pltpu.VMEM(gram.shape, jnp.float32),
            pltpu.SemaphoreType.DMA((count, win)),
            pltpu.SemaphoreType.DMA((count, win)),
            pltpu.SemaphoreType.DMA((count,)),
            pltpu.SemaphoreType.DMA((2 * steps,)),
            pltpu.SemaphoreType.DMA((2 * steps,)),
        ],
        compiler_params=pltpu.CompilerParams(
            collective_id=call_id, has_side_effects=True, vmem_limit_bytes=VMEM_BYTES
        ),
        name=f"share_{call_id}",
    )(gram, *payload)
    return result[0], result[1:]


def fold_kernel(devices, totals_ref, out_ref, box_ref, send_sem, recv_sem):
    me = lax.axis_index("dev")
    greet(devices, me, False)
    copies = []
    for place in range(1, len(OFFSETS)):
        copy = pltpu.make_async_remote_copy(
            src_ref=totals_ref.at[place],
            dst_ref=box_ref.at[place],
            send_sem=send_sem.at[place],
            recv_sem=recv_sem.at[place],
            device_id=((me + OFFSETS[place] + devices) % devices,),
            device_id_type=MESH_ID,
        )
        copy.start()
        copies.append(copy)
    for copy in copies:
        copy.wait()
    total = totals_ref[0]
    for place in range(1, len(OFFSETS)):
        total = total + box_ref[place]
    out_ref[...] = total


def fold(devices, call_id, totals):
    win = len(OFFSETS)
    return pl.pallas_call(
        functools.partial(fold_kernel, devices),
        out_shape=jax.ShapeDtypeStruct(totals.shape[1:], jnp.float32),
        in_specs=[VMEM_SPEC],
        out_specs=VMEM_SPEC,
        scratch_shapes=[
            pltpu.VMEM(totals.shape, jnp.float32),
            pltpu.SemaphoreType.DMA((win,)),
            pltpu.SemaphoreType.DMA((win,)),
        ],
        compiler_params=pltpu.CompilerParams(
            collective_id=call_id, has_side_effects=True, vmem_limit_bytes=VMEM_BYTES
        ),
        name=f"fold_{call_id}",
    )(totals)


def tile_kernel(mode, pos_ref, count_ref, tile_ref, left_ref, right_ref, out_ref, acc_ref):
    slot = pl.program_id(0)
    rows_first, rows_second, rows_third = tile_ref.shape[1:]
    rank = out_ref.shape[2]

    @pl.when(slot == 0)
    def _():
        out_ref[...] = jnp.zeros_like(out_ref)

    @pl.when(slot < count_ref[0])
    def _():
        at_left = pos_ref[slot, 0 if mode else 1]
        at_right = pos_ref[slot, 1 if mode == 2 else 2]
        for part in range(rank // LANES):
            lanes = slice(part * LANES, (part + 1) * LANES)
            right = right_ref[at_right, :, lanes]
            if mode == 0:
                left = left_ref[at_left, :, lanes].astype(jnp.float32)

                def row_step(group, carry):
                    base = pl.multiple_of(group * 8, 8)
                    sums = []
                    for i in range(8):
                        product = bf_dot(tile_ref[0, base + i], right)
                        sums.append(jnp.sum(product * left, axis=0, keepdims=True))
                    acc_ref[pl.ds(base, 8), lanes] = jnp.concatenate(sums, axis=0)
                    return carry

                lax.fori_loop(0, rows_first // 8, row_step, 0)
            else:
                acc_ref[0:rows_first, lanes] = left_ref[at_left, :, lanes].astype(jnp.float32)

                def row_add(group, total):
                    base = pl.multiple_of(group * 8, 8)
                    weights = acc_ref[pl.ds(base, 8), lanes]
                    for i in range(8):
                        if mode == 1:
                            product = bf_dot(tile_ref[0, base + i], right)
                        else:
                            product = lax.dot_general(
                                tile_ref[0, base + i],
                                right,
                                (((0,), (0,)), ((), ())),
                                preferred_element_type=jnp.float32,
                            )
                        total = total + product * weights[i : i + 1, :]
                    return total

                rows_out = rows_second if mode == 1 else rows_third
                total = lax.fori_loop(
                    0, rows_first // 8, row_add, jnp.zeros((rows_out, LANES), jnp.float32)
                )
                at_out = pos_ref[slot, mode]
                out_ref[at_out, :, lanes] += total
        if mode == 0:
            out_ref[pos_ref[slot, 0]] += acc_ref[...]


def tile_products(mode, positions, count, tiles, left, right):
    slots, rows_first, rows_second, rows_third = tiles.shape
    rank = left.shape[2]
    win = len(OFFSETS)
    rows_out = (rows_first, rows_second, rows_third)[mode]
    whole = lambda s, pos, cnt: (0, 0, 0)
    live = lambda s, pos, cnt: (jnp.minimum(s, cnt[0] - 1), 0, 0, 0)
    flops = 2 * tiles.size * rank
    return pl.pallas_call(
        functools.partial(tile_kernel, mode),
        out_shape=jax.ShapeDtypeStruct((win, rows_out, rank), jnp.float32),
        grid_spec=pltpu.PrefetchScalarGridSpec(
            num_scalar_prefetch=2,
            grid=(slots,),
            in_specs=[
                pl.BlockSpec((1, rows_first, rows_second, rows_third), live),
                pl.BlockSpec(left.shape, whole),
                pl.BlockSpec(right.shape, whole),
            ],
            out_specs=pl.BlockSpec((win, rows_out, rank), whole),
            scratch_shapes=[pltpu.VMEM((rows_first, rank), jnp.float32)],
        ),
        compiler_params=pltpu.CompilerParams(
            dimension_semantics=("arbitrary",), vmem_limit_bytes=VMEM_BYTES
        ),
        cost_estimate=pl.CostEstimate(
            flops=flops, bytes_accessed=2 * tiles.size, transcendentals=0
        ),
        name=f"tiles_{mode}",
    )(positions, count, tiles, left, right)


def split(value):
    high = value.astype(jnp.bfloat16)
    low = (value - high.astype(jnp.float32)).astype(jnp.bfloat16)
    return high, low


def admm_kernel(mode, starts, last, *refs):
    p1_ref, p2_ref, m_ref, h_ref, u_ref, weight_ref, h_out, u_out = refs[:8]
    if last:
        low_out = gram_out = None
        rest = refs[8:]
    else:
        low_out, gram_out = refs[8:10]
        rest = refs[10:]
    a_ref, x_ref, a_hi, a_lo, x_hi, x_lo, y_hi, y_lo = rest
    rank = h_ref.shape[2]
    weight = weight_ref[mode]
    block_rows = lax.broadcasted_iota(jnp.int32, (LANES, LANES), 0)
    block_cols = lax.broadcasted_iota(jnp.int32, (LANES, LANES), 1)
    on_diag = block_rows == block_cols
    trace = jnp.zeros((), jnp.float32)
    for index, (i, j) in enumerate(block_pairs(rank)):
        row = index * LANES
        one = p1_ref[starts[0] + row : starts[0] + row + LANES, :]
        two = p2_ref[starts[1] + row : starts[1] + row + LANES, :]
        block = one * two
        a_ref[i * LANES : (i + 1) * LANES, j * LANES : (j + 1) * LANES] = block
        if i == j:
            trace = trace + jnp.sum(jnp.where(on_diag, block, 0.0))
        else:
            a_ref[j * LANES : (j + 1) * LANES, i * LANES : (i + 1) * LANES] = block.T
    mean = trace / rank
    rho = weight * mean
    top = trace + rho
    low_end = weight / (rank + weight)
    scale = jnp.minimum(2.0 / (1.0 + low_end), 1.95)
    first = scale / top
    rows = lax.broadcasted_iota(jnp.int32, (LANES, rank), 0)
    cols = lax.broadcasted_iota(jnp.int32, (LANES, rank), 1)
    for i in range(rank // LANES):
        band = slice(i * LANES, (i + 1) * LANES)
        diag = rows + i * LANES == cols
        a = a_ref[band, :] + jnp.where(diag, rho, 0.0)
        a_ref[band, :] = a
        a_hi[band, :], a_lo[band, :] = split(a)
        x_ref[band, :] = jnp.where(diag, 2.0 * first, 0.0) - (first * first) * a

    def ends(low, scale):
        return jnp.minimum(scale * low * (2.0 - scale * low), scale * (2.0 - scale))

    def sweep(index, low):
        scale = jnp.minimum(2.0 / (1.0 + low), 1.95)
        for i in range(rank // LANES):
            band = slice(i * LANES, (i + 1) * LANES)
            x = x_ref[band, :] * scale
            x_ref[band, :] = x
            x_hi[band, :], x_lo[band, :] = split(x)
        for i in range(2):
            band = slice(i * (rank // 2), (i + 1) * (rank // 2))
            xh = x_hi[band, :]
            y = bf_dot(xh, a_hi[...]) + (bf_dot(xh, a_lo[...]) + bf_dot(x_lo[band, :], a_hi[...]))
            y_hi[band, :], y_lo[band, :] = split(y)
        for i in range(2):
            band = slice(i * (rank // 2), (i + 1) * (rank // 2))
            yh = y_hi[band, :]
            z = bf_dot(yh, x_hi[...]) + (bf_dot(yh, x_lo[...]) + bf_dot(y_lo[band, :], x_hi[...]))
            x_ref[band, :] = 2.0 * x_ref[band, :] - z
        return ends(low, scale)

    lax.fori_loop(0, 6, sweep, ends(low_end, scale))
    for i in range(rank // LANES):
        band = slice(i * LANES, (i + 1) * LANES)
        x_hi[band, :], x_lo[band, :] = split(x_ref[band, :])
        diag = rows + i * LANES == cols
        rest_of = jnp.where(diag, 1.0, 0.0) - f32_dot(x_ref[band, :], a_ref[...])
        y_hi[band, :] = rest_of.astype(jnp.bfloat16)
    x_ref[...] = x_ref[...] + bf_dot(y_hi[...], x_hi[...])

    mttkrp = m_ref[...]
    factor = h_ref[0]
    dual = u_ref[0]
    for sweep_index in range(ITERS):
        auxiliary = f32_dot(mttkrp + rho * (factor + dual), x_ref[...])
        factor = jnp.maximum(auxiliary - dual, 0.0)
        dual = dual + factor - auxiliary
    h_out[0] = factor
    u_out[0] = dual
    if not last:
        low_out[...] = factor.astype(jnp.bfloat16)
        place = write_gram(gram_out, 0, factor)
        if place < gram_out.shape[0]:
            gram_out[place:, :] = jnp.zeros((gram_out.shape[0] - place, LANES), jnp.float32)


def admm(mode, devices, packed, starts, mttkrp, factor, dual, penalty, last):
    rank = factor.shape[2]
    square = (rank, rank)
    out_shape = [
        jax.ShapeDtypeStruct(factor.shape, jnp.float32),
        jax.ShapeDtypeStruct(factor.shape, jnp.float32),
    ]
    if not last:
        out_shape += [
            jax.ShapeDtypeStruct(factor.shape[1:], jnp.bfloat16),
            jax.ShapeDtypeStruct((packed_rows(rank, 1, devices), LANES), jnp.float32),
        ]
    return pl.pallas_call(
        functools.partial(admm_kernel, mode, starts, last),
        out_shape=out_shape,
        in_specs=[VMEM_SPEC] * 5 + [SMEM_SPEC],
        out_specs=[VMEM_SPEC] * len(out_shape),
        scratch_shapes=[pltpu.VMEM(square, jnp.float32)] * 2
        + [pltpu.VMEM(square, jnp.bfloat16)] * 6,
        compiler_params=pltpu.CompilerParams(vmem_limit_bytes=VMEM_BYTES),
        name=f"admm_{mode}",
    )(packed[0], packed[1], mttkrp, factor, dual, penalty)


def per_device(
    devices,
    tensor_tiles,
    tile_coords,
    tile_count,
    owned_i,
    owned_j,
    owned_k,
    factor_a,
    factor_b,
    factor_c,
    dual_a,
    dual_b,
    dual_c,
    penalty,
):
    rank = factor_a.shape[2]
    one_gram = len(block_pairs(rank)) * LANES
    own_ids = jnp.broadcast_to(
        jnp.concatenate([owned_i, owned_j, owned_k, jnp.zeros((5,), jnp.int32)])[:, None],
        (8, LANES),
    )
    gram_bc, low_b, low_c = pl.pallas_call(
        gram_pair_kernel,
        out_shape=[
            jax.ShapeDtypeStruct((packed_rows(rank, 2, devices), LANES), jnp.float32),
            jax.ShapeDtypeStruct(factor_b.shape[1:], jnp.bfloat16),
            jax.ShapeDtypeStruct(factor_c.shape[1:], jnp.bfloat16),
        ],
        in_specs=[VMEM_SPEC] * 2,
        out_specs=[VMEM_SPEC] * 3,
        compiler_params=pltpu.CompilerParams(vmem_limit_bytes=VMEM_BYTES),
        name="gram_pair",
    )(factor_b, factor_c)
    gram_bc, (win_b, win_c, ids) = share(devices, 0, gram_bc, (low_b, low_c, own_ids))
    window_ids = ids[:, :3, 0]
    match = tile_coords[:, None, :] == window_ids[None, :, :]
    places = jnp.arange(len(OFFSETS), dtype=jnp.int32)[None, :, None]
    positions = jnp.sum(jnp.where(match, places, 0), axis=1)
    positions = jnp.minimum(positions, len(OFFSETS) - 1)

    totals = tile_products(0, positions, tile_count, tensor_tiles, win_b, win_c)
    mttkrp_a = fold(devices, 3, totals)
    factor_a_new, dual_a_new, low_a, gram_a = admm(
        0, devices, (gram_bc, gram_bc), (0, one_gram), mttkrp_a, factor_a, dual_a, penalty, False
    )
    gram_a, (win_a,) = share(devices, 1, gram_a, (low_a,))

    totals = tile_products(1, positions, tile_count, tensor_tiles, win_a, win_c)
    mttkrp_b = fold(devices, 4, totals)
    factor_b_new, dual_b_new, low_bn, gram_bn = admm(
        1, devices, (gram_a, gram_bc), (0, one_gram), mttkrp_b, factor_b, dual_b, penalty, False
    )
    gram_bn, (win_bn,) = share(devices, 2, gram_bn, (low_bn,))

    totals = tile_products(2, positions, tile_count, tensor_tiles, win_a, win_bn)
    mttkrp_c = fold(devices, 5, totals)
    factor_c_new, dual_c_new = admm(
        2, devices, (gram_a, gram_bn), (0, 0), mttkrp_c, factor_c, dual_c, penalty, True
    )
    return (factor_a_new, dual_a_new, factor_b_new, dual_b_new, factor_c_new, dual_c_new)


def solution(mesh):
    block = P("dev", None, None)
    return jax.shard_map(
        functools.partial(per_device, mesh.shape["dev"]),
        mesh=mesh,
        in_specs=(
            P("dev", None, None, None),
            P("dev", None),
            P("dev"),
            P("dev"),
            P("dev"),
            P("dev"),
            block,
            block,
            block,
            block,
            block,
            block,
            P(),
        ),
        out_specs=(block,) * 6,
        check_vma=False,
    )
```

time: 1010 us -> 377 us (0.37)
  other arithmetic: 422 us -> 0.88 us
  Pallas kernels: 0 us -> 372 us
  waiting for transfers between devices: 229 us -> 0 us
  matrix products: 125 us -> 0 us
  loops' own time: 79.9 us -> 0 us
  starting transfers between devices: 70.1 us -> 0 us
  local copies, waits for them, and re-layouts: 50.6 us -> 2.37 us
  between operations: 29 us -> 3.28 us
    pallas_call x0 -> x13, Pallas kernels: none -> 372 us  [the longest x3 146 us: share(): pl.pallas_call(functools.partial(share_kernel, devices, count), out_shape...]
    another operation x64 -> x0, other arithmetic: 365 us -> none  [the longest x44 238 us: admm_update(): chol_low = jnp.linalg.cholesky(gram_mat + rho_value * identity)]
    psum x3 -> x0, waiting for transfers between devices: 192 us -> none  [the longest x1 120 us: per_device(): gram_a = lax.psum(gram_local(factor_a_new), 'dev')]
    dot_general x34 -> x0, matrix products: 85.5 us -> none  [the longest x8 31.6 us: first_part(): jnp.dot(flat_tile, third_rows, preferred_element_type=jnp.float32)]
    another operation x6 -> x0, loops' own time: 79.9 us -> none  [the longest x1 26.6 us: per_device(): lax.fori_loop(0, count_live, mode_third, (jnp.zeros((win_count, rows_thir...]
    ppermute x32 -> x0, starting transfers between devices: 70 us -> none  [passed_along(): return lax.ppermute(block, axis, route)]
    another operation x60 -> x0, matrix products: 39.6 us -> none  [the longest x18 16.4 us: admm_update(): chol_low = jnp.linalg.cholesky(gram_mat + rho_value * identity)]
    reduce_sum x15 -> x1, other arithmetic: 38.2 us -> 0.21 us  [per_device(): positions = jnp.sum(jnp.where(match, places, 0), axis=1)]
  transfers between devices with their start and end apart: 35 -> 0, of which waited for: 16 -> 0; matrix products, arithmetic and copies ran while one was open for 10% -> 0% of each run, Pallas kernels for 0% -> 0%
where the time goes in v1:
time: 377 us; the launch traced here: 379 us
  Pallas kernels  372 us (99%)
    pallas_call x3, Pallas kernels, share(): pl.pallas_call(functools.partial(share_kernel, devices, count), out_shape...  146 us
    pallas_call x3, Pallas kernels, fold(): pl.pallas_call(functools.partial(fold_kernel, devices), out_shape=jax.Sha...  103 us
    pallas_call x3, Pallas kernels, admm(): pl.pallas_call(functools.partial(admm_kernel, mode, starts, last), out_sh...  62.7 us
    pallas_call x3, Pallas kernels, tile_products(): pl.pallas_call(functools.partial(tile_kernel, mode), out_shape=jax.ShapeD...  57.2 us

profile of v1, /device:TPU:0, one launch (start us, length us, event | category | flops | bytes accessed | tf_op | source)
XLA Modules:
  0.0 378.9 jit_solution(14430407784952384200)
XLA Ops:
  3.2 0.1 pad_add_fusion
  3.3 0.8 copy.21
  4.1 0.7 broadcast_in_dim.20.refs_3_
  4.7 3.3 gram_pair.1
  8.1 63.5 %share_0.1 = (f32[2560,128]{1,0:T(8,128)}, bf16[5,128,512]{2,1,0:T(8,128)(2,1)}, bf16[5,128,512]{2,1,0:T(8,128)(2,1)}, s32[5,8,128]{2,1,0:T(8,128)}) custom-call(f32[2560,128]{1,0:T(8,128)} %get-tuple-element.27.refs_0_, bf16[128,512]{1,0:T(8,128)(2,1)} %get-tuple-element.28.refs_1_, bf16[128,512]{1,0:T(8,128)(2,1)} %get-tuple-element.29.refs_2_, ...), custom_call_target="tpu_custom_call" | custom-call | tf_op jit(solution)/shard_map/share_0/pallas_call | solution.py:161
  71.6 0.7 slice.3
  72.3 0.1 copy.22
  72.4 0.2 select_reduce_fusion
  72.6 0.1 copy.23
  72.7 0.6 broadcast_minimum_fusion.pos_ref
  73.3 18.3 %tiles_0.1.totals_ref = f32[5,64,512]{2,1,0:T(8,128)} custom-call(s32[4,3]{1,0:T(4,128)} %broadcast_minimum_fusion.pos_ref, s32[1]{0:T(128)S(6)} %copy.24.count_ref, bf16[4,64,128,128]{3,2,1,0:T(8,128)(2,1)} %tile_ref.5, bf16[5,128,512]{2,1,0:T(8,128)(2,1)} %get-tuple-element.32.left_ref, bf16[5,128,512]{2,1,0:T(8,128)(2,1)} %get-tuple-element.33.right_ref), custom_call_target="tpu_custom_call" | custom-call | flops 4294967296 | bytes 8388608 | tf_op jit(solution)/shard_map/tiles_0/pallas_call | solution.py:292
  91.7 28.4 %fold_3.1.refs_2_ = f32[64,512]{1,0:T(8,128)} custom-call(f32[5,64,512]{2,1,0:T(8,128)} %tiles_0.1.totals_ref), custom_call_target="tpu_custom_call" | custom-call | tf_op jit(solution)/shard_map/fold_3/pallas_call | solution.py:209
  120.1 21.6 %admm_0.1 = (f32[1,64,512]{2,1,0:T(8,128)}, f32[1,64,512]{2,1,0:T(8,128)}, bf16[64,512]{1,0:T(8,128)(2,1)}, f32[1280,128]{1,0:T(8,128)}) custom-call(f32[2560,128]{1,0:T(8,128)} %get-tuple-element.30.refs_0_.refs_1_, f32[2560,128]{1,0:T(8,128)} %get-tuple-element.30.refs_0_.refs_1_, f32[64,512]{1,0:T(8,128)} %fold_3.1.refs_2_, f32[1,64,512]{2,1,0:T(8,128)} %refs_3_.3, ...), custom_call_target="tpu_custom_call" | custom-call | tf_op jit(solution)/shard_map/admm_0/pallas_call | solution.py:422
  141.7 39.2 %share_1.1 = (f32[1280,128]{1,0:T(8,128)}, bf16[5,64,512]{2,1,0:T(8,128)(2,1)}) custom-call(f32[1280,128]{1,0:T(8,128)} %get-tuple-element.36.refs_0_, bf16[64,512]{1,0:T(8,128)(2,1)} %get-tuple-element.37.refs_1_), custom_call_target="tpu_custom_call" | custom-call | tf_op jit(solution)/shard_map/share_1/pallas_call | solution.py:161
  180.8 18.0 %tiles_1.1.totals_ref = f32[5,128,512]{2,1,0:T(8,128)} custom-call(s32[4,3]{1,0:T(4,128)} %broadcast_minimum_fusion.pos_ref, s32[1]{0:T(128)S(6)} %copy.24.count_ref, bf16[4,64,128,128]{3,2,1,0:T(8,128)(2,1)} %tile_ref.5, bf16[5,64,512]{2,1,0:T(8,128)(2,1)} %get-tuple-element.39.left_ref, bf16[5,128,512]{2,1,0:T(8,128)(2,1)} %get-tuple-element.33.right_ref), custom_call_target="tpu_custom_call" | custom-call | flops 4294967296 | bytes 8388608 | tf_op jit(solution)/shard_map/tiles_1/pallas_call | solution.py:292
  198.9 35.2 %fold_4.1.refs_2_ = f32[128,512]{1,0:T(8,128)} custom-call(f32[5,128,512]{2,1,0:T(8,128)} %tiles_1.1.totals_ref), custom_call_target="tpu_custom_call" | custom-call | tf_op jit(solution)/shard_map/fold_4/pallas_call | solution.py:209
  234.1 21.0 %admm_1.1 = (f32[1,128,512]{2,1,0:T(8,128)}, f32[1,128,512]{2,1,0:T(8,128)}, bf16[128,512]{1,0:T(8,128)(2,1)}, f32[1280,128]{1,0:T(8,128)}) custom-call(f32[1280,128]{1,0:T(8,128)} %get-tuple-element.38.refs_0_, f32[2560,128]{1,0:T(8,128)} %get-tuple-element.30.refs_0_.refs_1_, f32[128,512]{1,0:T(8,128)} %fold_4.1.refs_2_, f32[1,128,512]{2,1,0:T(8,128)} %refs_3_.4, ...), custom_call_target="tpu_custom_call" | custom-call | tf_op jit(solution)/shard_map/admm_1/pallas_call | solution.py:422
  255.1 43.5 %share_2.1 = (f32[1280,128]{1,0:T(8,128)}, bf16[5,128,512]{2,1,0:T(8,128)(2,1)}) custom-call(f32[1280,128]{1,0:T(8,128)} %get-tuple-element.42.refs_0_, bf16[128,512]{1,0:T(8,128)(2,1)} %get-tuple-element.43.refs_1_), custom_call_target="tpu_custom_call" | custom-call | tf_op jit(solution)/shard_map/share_2/pallas_call | solution.py:161
  298.6 20.8 %tiles_2.1.totals_ref = f32[5,128,512]{2,1,0:T(8,128)} custom-call(s32[4,3]{1,0:T(4,128)} %broadcast_minimum_fusion.pos_ref, s32[1]{0:T(128)S(6)} %copy.24.count_ref, bf16[4,64,128,128]{3,2,1,0:T(8,128)(2,1)} %tile_ref.5, bf16[5,64,512]{2,1,0:T(8,128)(2,1)} %get-tuple-element.39.left_ref, bf16[5,128,512]{2,1,0:T(8,128)(2,1)} %get-tuple-element.45.right_ref), custom_call_target="tpu_custom_call" | custom-call | flops 4294967296 | bytes 8388608 | tf_op jit(solution)/shard_map/tiles_2/pallas_call | solution.py:292
  319.4 39.4 %fold_5.1.refs_2_ = f32[128,512]{1,0:T(8,128)} custom-call(f32[5,128,512]{2,1,0:T(8,128)} %tiles_2.1.totals_ref), custom_call_target="tpu_custom_call" | custom-call | tf_op jit(solution)/shard_map/fold_5/pallas_call | solution.py:209
  358.8 20.1 %admm_2.1 = (f32[1,128,512]{2,1,0:T(8,128)}, f32[1,128,512]{2,1,0:T(8,128)}) custom-call(f32[1280,128]{1,0:T(8,128)} %get-tuple-element.38.refs_0_, f32[1280,128]{1,0:T(8,128)} %get-tuple-element.44.refs_1_, f32[128,512]{1,0:T(8,128)} %fold_5.1.refs_2_, f32[1,128,512]{2,1,0:T(8,128)} %refs_3_.5, f32[1,128,512]{2,1,0:T(8,128)} %refs_4_.5, f32[3]{0:T(128)} %refs_5_.5), custom_call_target="tpu_custom_call" | custom-call | tf_op jit(solution)/shard_map/admm_2/pallas_call | solution.py:422
  (1 shorter events, 0.0 us)

commit v2 on v1

--- a/solution.py
+++ b/solution.py
@@ -10,6 +10,7 @@
 ITERS = 6
 REACH = 2
 LANES = 128
+WIDE = 256
 MESH_ID = pl.DeviceIdType.MESH
 HIGHEST = lax.Precision.HIGHEST
 VMEM_SPEC = pl.BlockSpec(memory_space=pltpu.VMEM)
@@ -67,12 +68,23 @@
     low_c_ref[...] = c_ref[0].astype(jnp.bfloat16)
 
 
+def cube_levels(devices):
+    levels = []
+    stride = 1
+    while stride < devices:
+        radix = 2 if stride == 1 or devices // stride % 4 else 4
+        levels.append((radix, stride))
+        stride *= radix
+    return levels
+
+
 def greet(devices, me, with_cube):
     others = []
     if with_cube:
-        for t in range(devices.bit_length() - 1):
-            bit = (me // (1 << t)) % 2
-            others.append(me + (1 - 2 * bit) * (1 << t))
+        for radix, stride in cube_levels(devices):
+            digit = (me // stride) % radix
+            for turn in range(1, radix):
+                others.append(me + ((digit + turn) % radix - digit) * stride)
     for offset in OFFSETS[1:]:
         others.append((me + offset + devices) % devices)
     barrier = pltpu.get_barrier_semaphore()
@@ -89,73 +101,85 @@
     box_ref, part_ref, win_send, win_recv, local_sem, cube_send, cube_recv = refs[2 + 2 * payloads :]
     me = lax.axis_index("dev")
     greet(devices, me, True)
+    levels = cube_levels(devices)
+    length = gram_ref.shape[0]
+    start = 0
+    box = 0
     window_copies = []
-    for place in range(1, len(OFFSETS)):
-        target = (me - OFFSETS[place] + devices) % devices
-        for q in range(payloads):
+    for level, (radix, stride) in enumerate(levels):
+        piece = length // radix
+        digit = (me // stride) % radix
+        source = gram_ref if level == 0 else part_ref
+        target = sum_ref if level == len(levels) - 1 else part_ref
+        copies = []
+        for turn in range(1, radix):
+            other = (digit + turn) % radix
+            give = pl.multiple_of(start + other * piece, 8)
             copy = pltpu.make_async_remote_copy(
-                src_ref=own_refs[q],
-                dst_ref=win_refs[q].at[place],
-                send_sem=win_send.at[q, place],
-                recv_sem=win_recv.at[q, place],
-                device_id=(target,),
+                src_ref=source.at[pl.ds(give, piece)],
+                dst_ref=box_ref.at[pl.ds(box + (turn - 1) * piece, piece)],
+                send_sem=cube_send.at[level, turn],
+                recv_sem=cube_recv.at[level, turn],
+                device_id=(me + (other - digit) * stride,),
                 device_id_type=MESH_ID,
             )
             copy.start()
-            window_copies.append(copy)
-    for q in range(payloads):
-        own = pltpu.make_async_copy(own_refs[q], win_refs[q].at[0], local_sem.at[q])
-        own.start()
-        window_copies.append(own)
-
-    steps = devices.bit_length() - 1
-    length = gram_ref.shape[0]
-    start = 0
-    box = 0
-    for t in range(steps):
-        half = length // 2
-        bit = (me // (1 << t)) % 2
-        partner = me + (1 - 2 * bit) * (1 << t)
-        keep = pl.multiple_of(start + bit * half, 8)
-        give = pl.multiple_of(start + (1 - bit) * half, 8)
-        source = gram_ref if t == 0 else part_ref
-        target = sum_ref if t == steps - 1 else part_ref
-        copy = pltpu.make_async_remote_copy(
-            src_ref=source.at[pl.ds(give, half)],
-            dst_ref=box_ref.at[pl.ds(box, half)],
-            send_sem=cube_send.at[t],
-            recv_sem=cube_recv.at[t],
-            device_id=(partner,),
-            device_id_type=MESH_ID,
-        )
-        copy.start()
-        copy.wait()
-        target[pl.ds(keep, half), :] = source[pl.ds(keep, half), :] + box_ref[pl.ds(box, half), :]
-        box += half
+            copies.append(copy)
+        if level == 0:
+            for place in range(1, len(OFFSETS)):
+                window_to = (me - OFFSETS[place] + devices) % devices
+                for q in range(payloads):
+                    copy = pltpu.make_async_remote_copy(
+                        src_ref=own_refs[q],
+                        dst_ref=win_refs[q].at[place],
+                        send_sem=win_send.at[q, place],
+                        recv_sem=win_recv.at[q, place],
+                        device_id=(window_to,),
+                        device_id_type=MESH_ID,
+                    )
+                    copy.start()
+                    window_copies.append(copy)
+            for q in range(payloads):
+                own = pltpu.make_async_copy(own_refs[q], win_refs[q].at[0], local_sem.at[q])
+                own.start()
+                window_copies.append(own)
+        for copy in copies:
+            copy.wait()
+        keep = pl.multiple_of(start + digit * piece, 8)
+        total = source[pl.ds(keep, piece), :]
+        for turn in range(1, radix):
+            total = total + box_ref[box + (turn - 1) * piece : box + turn * piece, :]
+        target[pl.ds(keep, piece), :] = total
+        box += (radix - 1) * piece
         start = keep
-        length = half
-    for t in reversed(range(steps)):
-        bit = (me // (1 << t)) % 2
-        partner = me + (1 - 2 * bit) * (1 << t)
+        length = piece
+    for level in reversed(range(len(levels))):
+        radix, stride = levels[level]
+        digit = (me // stride) % radix
         piece = pl.ds(pl.multiple_of(start, 8), length)
-        copy = pltpu.make_async_remote_copy(
-            src_ref=sum_ref.at[piece],
-            dst_ref=sum_ref.at[piece],
-            send_sem=cube_send.at[steps + t],
-            recv_sem=cube_recv.at[steps + t],
-            device_id=(partner,),
-            device_id_type=MESH_ID,
-        )
-        copy.start()
-        copy.wait()
-        start = start - bit * length
-        length = 2 * length
+        copies = []
+        for turn in range(1, radix):
+            other = (digit + turn) % radix
+            copy = pltpu.make_async_remote_copy(
+                src_ref=sum_ref.at[piece],
+                dst_ref=sum_ref.at[piece],
+                send_sem=cube_send.at[len(levels) + level, turn],
+                recv_sem=cube_recv.at[len(levels) + level, turn],
+                device_id=(me + (other - digit) * stride,),
+                device_id_type=MESH_ID,
+            )
+            copy.start()
+            copies.append(copy)
+        for copy in copies:
+            copy.wait()
+        start = start - digit * length
+        length = radix * length
     for copy in window_copies:
         copy.wait()
 
 
 def share(devices, call_id, gram, payload):
-    steps = devices.bit_length() - 1
+    phases = 2 * len(cube_levels(devices))
     win = len(OFFSETS)
     count = len(payload)
     result = pl.pallas_call(
@@ -170,8 +194,8 @@
             pltpu.SemaphoreType.DMA((count, win)),
             pltpu.SemaphoreType.DMA((count, win)),
             pltpu.SemaphoreType.DMA((count,)),
-            pltpu.SemaphoreType.DMA((2 * steps,)),
-            pltpu.SemaphoreType.DMA((2 * steps,)),
+            pltpu.SemaphoreType.DMA((phases, 4)),
+            pltpu.SemaphoreType.DMA((phases, 4)),
         ],
         compiler_params=pltpu.CompilerParams(
             collective_id=call_id, has_side_effects=True, vmem_limit_bytes=VMEM_BYTES
@@ -236,8 +260,9 @@
     def _():
         at_left = pos_ref[slot, 0 if mode else 1]
         at_right = pos_ref[slot, 1 if mode == 2 else 2]
-        for part in range(rank // LANES):
-            lanes = slice(part * LANES, (part + 1) * LANES)
+        wide = min(WIDE, rank)
+        for part in range(rank // wide):
+            lanes = slice(part * wide, (part + 1) * wide)
             right = right_ref[at_right, :, lanes]
             if mode == 0:
                 left = left_ref[at_left, :, lanes].astype(jnp.float32)
@@ -273,7 +298,7 @@
 
                 rows_out = rows_second if mode == 1 else rows_third
                 total = lax.fori_loop(
-                    0, rows_first // 8, row_add, jnp.zeros((rows_out, LANES), jnp.float32)
+                    0, rows_first // 8, row_add, jnp.zeros((rows_out, wide), jnp.float32)
                 )
                 at_out = pos_ref[slot, mode]
                 out_ref[at_out, :, lanes] += total

time: 377 us -> 315 us (0.84)
  Pallas kernels: 372 us -> 308 us
    pallas_call x3, Pallas kernels: 146 us -> 112 us  [share(): pl.pallas_call(functools.partial(share_kernel, devices, count), out_shape...]
    pallas_call x3, Pallas kernels: 57.2 us -> 40.8 us  [tile_products(): pl.pallas_call(functools.partial(tile_kernel, mode), out_shape=jax.ShapeD...]
    pallas_call x3, Pallas kernels: 103 us -> 89.7 us  [fold(): pl.pallas_call(functools.partial(fold_kernel, devices), out_shape=jax.Sha...]
where the time goes in v2:
time: 315 us
  Pallas kernels  308 us (98%)
  between operations  3.28 us (1%)
    pallas_call x3, Pallas kernels, share(): pl.pallas_call(functools.partial(share_kernel, devices, count), out_shape...  112 us
    pallas_call x3, Pallas kernels, fold(): pl.pallas_call(functools.partial(fold_kernel, devices), out_shape=jax.Sha...  89.7 us
    pallas_call x3, Pallas kernels, admm(): pl.pallas_call(functools.partial(admm_kernel, mode, starts, last), out_sh...  62.7 us
    pallas_call x3, Pallas kernels, tile_products(): pl.pallas_call(functools.partial(tile_kernel, mode), out_shape=jax.ShapeD...  40.8 us

profile of v2, /device:TPU:0, one launch (start us, length us, event | category | flops | bytes accessed | tf_op | source)
XLA Modules:
  0.0 314.8 jit_solution(3670347366587220959)
XLA Ops:
  3.2 0.1 pad_add_fusion
  3.3 0.8 copy.21
  4.1 0.7 broadcast_in_dim.20.refs_3_
  4.7 3.3 %gram_pair.1 = (f32[2560,128]{1,0:T(8,128)}, bf16[128,512]{1,0:T(8,128)(2,1)}, bf16[128,512]{1,0:T(8,128)(2,1)}) custom-call(f32[1,128,512]{2,1,0:T(8,128)} %refs_3_.4, f32[1,128,512]{2,1,0:T(8,128)} %refs_3_.5), custom_call_target="tpu_custom_call" | custom-call | tf_op jit(solution)/shard_map/gram_pair/pallas_call | solution.py:481
  8.1 52.8 %share_0.1 = (f32[2560,128]{1,0:T(8,128)}, bf16[5,128,512]{2,1,0:T(8,128)(2,1)}, bf16[5,128,512]{2,1,0:T(8,128)(2,1)}, s32[5,8,128]{2,1,0:T(8,128)}) custom-call(f32[2560,128]{1,0:T(8,128)} %get-tuple-element.27.refs_0_, bf16[128,512]{1,0:T(8,128)(2,1)} %get-tuple-element.28.refs_1_, bf16[128,512]{1,0:T(8,128)(2,1)} %get-tuple-element.29.refs_2_, ...), custom_call_target="tpu_custom_call" | custom-call | tf_op jit(solution)/shard_map/share_0/pallas_call | solution.py:185
  60.8 0.7 slice.3
  61.5 0.1 copy.22
  61.7 0.2 select_reduce_fusion
  61.9 0.1 copy.23
  62.0 0.6 broadcast_minimum_fusion.pos_ref
  62.6 13.1 %tiles_0.1.totals_ref = f32[5,64,512]{2,1,0:T(8,128)} custom-call(s32[4,3]{1,0:T(4,128)} %broadcast_minimum_fusion.pos_ref, s32[1]{0:T(128)S(6)} %copy.24.count_ref, bf16[4,64,128,128]{3,2,1,0:T(8,128)(2,1)} %tile_ref.5, bf16[5,128,512]{2,1,0:T(8,128)(2,1)} %get-tuple-element.32.left_ref, bf16[5,128,512]{2,1,0:T(8,128)(2,1)} %get-tuple-element.33.right_ref), custom_call_target="tpu_custom_call" | custom-call | flops 4294967296 | bytes 8388608 | tf_op jit(solution)/shard_map/tiles_0/pallas_call | solution.py:317
  75.7 24.1 %fold_3.1.refs_2_ = f32[64,512]{1,0:T(8,128)} custom-call(f32[5,64,512]{2,1,0:T(8,128)} %tiles_0.1.totals_ref), custom_call_target="tpu_custom_call" | custom-call | tf_op jit(solution)/shard_map/fold_3/pallas_call | solution.py:233
  99.8 21.6 %admm_0.1 = (f32[1,64,512]{2,1,0:T(8,128)}, f32[1,64,512]{2,1,0:T(8,128)}, bf16[64,512]{1,0:T(8,128)(2,1)}, f32[1280,128]{1,0:T(8,128)}) custom-call(f32[2560,128]{1,0:T(8,128)} %get-tuple-element.30.refs_0_.refs_1_, f32[2560,128]{1,0:T(8,128)} %get-tuple-element.30.refs_0_.refs_1_, f32[64,512]{1,0:T(8,128)} %fold_3.1.refs_2_, f32[1,64,512]{2,1,0:T(8,128)} %refs_3_.3, ...), custom_call_target="tpu_custom_call" | custom-call | tf_op jit(solution)/shard_map/admm_0/pallas_call | solution.py:447
  121.4 27.5 %share_1.1 = (f32[1280,128]{1,0:T(8,128)}, bf16[5,64,512]{2,1,0:T(8,128)(2,1)}) custom-call(f32[1280,128]{1,0:T(8,128)} %get-tuple-element.36.refs_0_, bf16[64,512]{1,0:T(8,128)(2,1)} %get-tuple-element.37.refs_1_), custom_call_target="tpu_custom_call" | custom-call | tf_op jit(solution)/shard_map/share_1/pallas_call | solution.py:185
  148.9 13.1 %tiles_1.1.totals_ref = f32[5,128,512]{2,1,0:T(8,128)} custom-call(s32[4,3]{1,0:T(4,128)} %broadcast_minimum_fusion.pos_ref, s32[1]{0:T(128)S(6)} %copy.24.count_ref, bf16[4,64,128,128]{3,2,1,0:T(8,128)(2,1)} %tile_ref.5, bf16[5,64,512]{2,1,0:T(8,128)(2,1)} %get-tuple-element.39.left_ref, bf16[5,128,512]{2,1,0:T(8,128)(2,1)} %get-tuple-element.33.right_ref), custom_call_target="tpu_custom_call" | custom-call | flops 4294967296 | bytes 8388608 | tf_op jit(solution)/shard_map/tiles_1/pallas_call | solution.py:317
  162.0 32.0 %fold_4.1.refs_2_ = f32[128,512]{1,0:T(8,128)} custom-call(f32[5,128,512]{2,1,0:T(8,128)} %tiles_1.1.totals_ref), custom_call_target="tpu_custom_call" | custom-call | tf_op jit(solution)/shard_map/fold_4/pallas_call | solution.py:233
  194.1 21.0 %admm_1.1 = (f32[1,128,512]{2,1,0:T(8,128)}, f32[1,128,512]{2,1,0:T(8,128)}, bf16[128,512]{1,0:T(8,128)(2,1)}, f32[1280,128]{1,0:T(8,128)}) custom-call(f32[1280,128]{1,0:T(8,128)} %get-tuple-element.38.refs_0_, f32[2560,128]{1,0:T(8,128)} %get-tuple-element.30.refs_0_.refs_1_, f32[128,512]{1,0:T(8,128)} %fold_4.1.refs_2_, f32[1,128,512]{2,1,0:T(8,128)} %refs_3_.4, ...), custom_call_target="tpu_custom_call" | custom-call | tf_op jit(solution)/shard_map/admm_1/pallas_call | solution.py:447
  215.1 31.5 %share_2.1 = (f32[1280,128]{1,0:T(8,128)}, bf16[5,128,512]{2,1,0:T(8,128)(2,1)}) custom-call(f32[1280,128]{1,0:T(8,128)} %get-tuple-element.42.refs_0_, bf16[128,512]{1,0:T(8,128)(2,1)} %get-tuple-element.43.refs_1_), custom_call_target="tpu_custom_call" | custom-call | tf_op jit(solution)/shard_map/share_2/pallas_call | solution.py:185
  246.6 14.5 %tiles_2.1.totals_ref = f32[5,128,512]{2,1,0:T(8,128)} custom-call(s32[4,3]{1,0:T(4,128)} %broadcast_minimum_fusion.pos_ref, s32[1]{0:T(128)S(6)} %copy.24.count_ref, bf16[4,64,128,128]{3,2,1,0:T(8,128)(2,1)} %tile_ref.5, bf16[5,64,512]{2,1,0:T(8,128)(2,1)} %get-tuple-element.39.left_ref, bf16[5,128,512]{2,1,0:T(8,128)(2,1)} %get-tuple-element.45.right_ref), custom_call_target="tpu_custom_call" | custom-call | flops 4294967296 | bytes 8388608 | tf_op jit(solution)/shard_map/tiles_2/pallas_call | solution.py:317
  261.1 33.6 %fold_5.1.refs_2_ = f32[128,512]{1,0:T(8,128)} custom-call(f32[5,128,512]{2,1,0:T(8,128)} %tiles_2.1.totals_ref), custom_call_target="tpu_custom_call" | custom-call | tf_op jit(solution)/shard_map/fold_5/pallas_call | solution.py:233
  294.7 20.1 %admm_2.1 = (f32[1,128,512]{2,1,0:T(8,128)}, f32[1,128,512]{2,1,0:T(8,128)}) custom-call(f32[1280,128]{1,0:T(8,128)} %get-tuple-element.38.refs_0_, f32[1280,128]{1,0:T(8,128)} %get-tuple-element.44.refs_1_, f32[128,512]{1,0:T(8,128)} %fold_5.1.refs_2_, f32[1,128,512]{2,1,0:T(8,128)} %refs_3_.5, f32[1,128,512]{2,1,0:T(8,128)} %refs_4_.5, f32[3]{0:T(128)} %refs_5_.5), custom_call_target="tpu_custom_call" | custom-call | tf_op jit(solution)/shard_map/admm_2/pallas_call | solution.py:447
  (1 shorter events, 0.0 us)
